TPU v7x, 32 devices: a whole 2x2x4 slice. The times are simulated.
32 devices in a mesh: grp: 8 (over z, core), blk: 4 (over y, x).
Axes of the slice: x: 2, y: 2, z: 4, core: 2. Of those that a mesh axis runs over, the one named last changes fastest.
Arguments:
- slab: bfloat16 [2048, 32768], P(('grp', 'blk')), as said below
- pick_owner: int32 [2048, 1], P(('grp', 'blk')), may hold values from 0 to 3; in each aligned block of 64 rows (0 to 63, 64 to 127, ...) at most 32 rows name the same one
- pick_offset: int32 [2048], P(('grp', 'blk')), may hold values from 0 to 63
- wedge_id: int32 [2048], P(('grp', 'blk')), may hold values from 0 to 7
- live_count: int32 [32], P(('grp', 'blk')), may hold values from 16 to 64, as said below
- references: bfloat16 [192, 32768], P('blk')
- wedge: float32 [8, 32768], replicated, may hold values from 0.05 to 1
Outputs:
- new_refs: float32 [192, 32768], P('blk', 'grp')
Inputs may be any that keep to these rules, and one draw needn't show every extreme that they name: `pick_owner`: on one device at most 32 slots name the same owner. `live_count`: live slots are the first ones of a device; some device has all 64 live. `slab`: coefficients of the tomogram blocks.
All inputs are finite; a program needn't handle non-finite values.
Results may differ from a plain program's by a relative error of at most 0.0036.
Values may be sent and summed in bfloat16 or wider, within the bound.
No kernel may reach another device: no remote copies, remote signals or barrier semaphores. Data moves between devices by JAX's collectives and lax.ppermute only.
A program may use at most 128 MiB of HBM per device.

v0:
```python
import math
import jax
import jax.numpy as jnp
from jax import lax
from jax.sharding import PartitionSpec as P


def per_device(slab, pick_owner, pick_offset, wedge_id, live_count, references, wedge):
    highest = lax.Precision.HIGHEST
    slot_count, voxels = slab.shape
    group_count = lax.axis_size("grp")
    cycle_size = lax.axis_size("blk")
    capacity = 2 * slot_count // cycle_size
    owners = pick_owner[:, 0]
    owner_hot = (owners[:, None] == jnp.arange(cycle_size, dtype=jnp.int32)[None, :]).astype(
        jnp.int32
    )
    slot_rank = jnp.sum((jnp.cumsum(owner_hot, axis=0) - 1) * owner_hot, axis=1)
    requests = jnp.zeros((cycle_size, capacity), jnp.int32).at[owners, slot_rank].set(pick_offset)
    wanted = lax.all_to_all(requests, "blk", split_axis=0, concat_axis=0, tiled=True)
    amount = wanted.shape[1]
    blocks_out = jnp.take(slab, wanted.reshape(-1), axis=0).reshape(cycle_size, amount, voxels)
    fetched = lax.all_to_all(blocks_out, "blk", split_axis=0, concat_axis=0, tiled=True)
    blocks = fetched[owners, slot_rank]
    masks_hot = (wedge_id[:, None] == jnp.arange(wedge.shape[0], dtype=jnp.int32)[None, :]).astype(
        jnp.float32
    )
    weights = jnp.dot(masks_hot, wedge, precision=highest)
    scaled = (weights * blocks.astype(jnp.float32)).astype(jnp.bfloat16)
    per_ref = references.shape[0]
    inv_noise = 1.0 / (32.0 * math.sqrt(voxels))
    ref_piece = lax.all_gather(references, "blk", axis=0, tiled=True)
    correl = jnp.dot(scaled, ref_piece.T, preferred_element_type=jnp.float32)
    piece_float = ref_piece.astype(jnp.float32)
    piece_norms = jnp.dot(wedge, (piece_float * piece_float).T, precision=highest)
    chosen_norms = jnp.dot(masks_hot, piece_norms, precision=highest)
    folded = correl - 0.5 * chosen_norms
    posterior = jax.nn.softmax(folded * inv_noise, axis=1)
    live_mask = (jnp.arange(slot_count, dtype=jnp.int32) < live_count[0]).astype(jnp.float32)
    weighted = posterior * live_mask[:, None]
    weighted_b = weighted.astype(jnp.bfloat16)
    totals = lax.psum(jnp.dot(weighted.T, masks_hot, precision=highest), ("grp", "blk"))
    per_vox = voxels // group_count
    contract = (((0,), (0,)), ((), ()))
    columns = lax.all_to_all(scaled, "grp", split_axis=1, concat_axis=0, tiled=True)
    all_weights = lax.all_gather(weighted_b, "grp", axis=0, tiled=True)
    summed = lax.psum_scatter(
        lax.dot_general(all_weights, columns, contract, preferred_element_type=jnp.float32),
        "blk",
        scatter_dimension=0,
        tiled=True,
    )
    row_first = lax.axis_index("blk") * per_ref
    vox_first = lax.axis_index("grp") * per_vox
    own_totals = lax.dynamic_slice_in_dim(totals, row_first, per_ref, 0)
    wedge_cols = lax.dynamic_slice_in_dim(wedge, vox_first, per_vox, 1)
    weight_sum = jnp.dot(own_totals, wedge_cols, precision=highest)
    return summed / (weight_sum + 1.0)


def solution(mesh):
    placed = (
        P(("grp", "blk"), None),
        P(("grp", "blk"), None),
        P(("grp", "blk")),
        P(("grp", "blk")),
        P(("grp", "blk")),
        P("blk", None),
        P(),
    )
    return jax.shard_map(
        per_device, mesh=mesh, in_specs=placed, out_specs=P("blk", "grp"), check_vma=False
    )
```

profile of v0, /device:TPU:0, one launch (start us, length us, event | category | flops | bytes accessed | tf_op | source)
XLA Modules:
  0.0 415.6 jit_solution(10837172099122750557)
XLA Ops:
  6.5 0.0 copy-start
  6.5 0.8 fusion.9
  7.4 0.1 reduce_window_sum.11
  7.4 0.8 select_reduce_fusion
  8.3 0.7 fusion.18
  9.0 0.6 broadcast_in_dim.12
  9.5 10.1 %scatter_fusion = s32[4,32]{1,0:T(4,128)} fusion(s32[4,32]{1,0:T(4,128)} %broadcast_in_dim.12, s32[64]{0:T(128)S(1)} %get-tuple-element.7, s32[64]{0:T(128)} %param.9), kind=kCustom, calls=%fused_computation.2 | custom fusion | bytes 1280 | tf_op jit(solution)/shard_map/scatter | solution.py:19
  19.7 5.2 %all-to-all-start = ((s32[4,1,32]{2,1,0:T(1,128)}), s32[4,1,32]{2,1,0:T(1,128)S(1)}, u32[]{:S(2)}, u32[]{:S(2)}) async-start(s32[4,1,32]{2,1,0:T(1,128)} %bitcast.4), calls=%async_computation | async-start | bytes 4096 | tf_op jit(solution)/shard_map/all_to_all | solution.py:20
  24.9 0.0 all-gather.2.cloned.1.call-start
  24.9 0.7 all-gather.2.cloned.1.call-update
  25.6 3.9 all-to-all-done
  29.5 0.5 broadcast.140
  30.0 0.7 reduce.3
  30.6 0.1 reshape.75
  30.7 19.2 %gather_fusion = bf16[128,32768]{1,0:T(8,128)(2,1)} fusion(bf16[64,32768]{1,0:T(8,128)(2,1)} %param.7, s32[1024]{0:T(1024)S(1)} %pad_clamp_fusion), kind=kCustom, calls=%fused_computation | custom fusion | bytes 16777728 | tf_op jit(solution)/shard_map/jit(_take)/gather | solution.py:22
  49.9 7.4 %broadcast_select_fusion = bf16[4,32,32768]{2,1,0:T(8,128)(2,1)} fusion(bf16[4,32,32768]{2,1,0:T(8,128)(2,1)} %bitcast.36, pred[4,32]{1,0:T(4,128)(4,1)S(1)} %compare_and_fusion), kind=kLoop, calls=%fused_computation.8 | loop fusion | flops 4194304 | bytes 16777344 | tf_op jit(solution)/shard_map/jit(_take)/select_n | solution.py:22
  57.4 171.9 %all_to_all.33 = bf16[4,32,32768]{2,1,0:T(8,128)(2,1)} all-to-all(bf16[4,32,32768]{2,1,0:T(8,128)(2,1)} %broadcast_select_fusion), channel_id=1, replica_groups=mesh['grp'=8,'blk'=4] {'blk'}, dimensions={0} | all-to-all | bytes 16777216 | tf_op jit(solution)/shard_map/all_to_all | solution.py:23
  229.3 0.0 copy-start.3
  229.3 12.2 %gather_fusion.1 = bf16[64,32768]{1,0:T(8,128)(2,1)} fusion(bf16[4,32,32768]{2,1,0:T(8,128)(2,1)} %all_to_all.33, s32[64]{0:T(128)S(1)} %bitcast.38), kind=kCustom, calls=%fused_computation.1 | custom fusion | bytes 8389120 | tf_op jit(solution)/shard_map/gather | solution.py:24
  241.5 0.0 copy-done
  241.5 0.0 copy-done.3
  241.5 5.5 %fusion = bf16[64,32768]{1,0:T(8,128)(2,1)S(1)} fusion(f32[8,32768]{1,0:T(8,128)S(1)} %copy-done, bf16[64,32768]{1,0:T(8,128)(2,1)} %gather_fusion.1, s32[64]{0:T(128)S(1)} %copy-done.3), kind=kOutput, calls=%fused_computation.4 | convolution fusion | flops 207618560 | bytes 9437440 | tf_op jit(solution)/shard_map/dot_general | solution.py:28
  247.0 0.0 copy-start.1
  247.0 2.0 copy-done.1
  249.0 2.2 copy.13
  251.2 4.6 %all-to-all-start.2 = ((bf16[64,8,4096]{2,0,1:T(8,128)(2,1)}), bf16[64,8,4096]{2,0,1:T(8,128)(2,1)}, u32[]{:S(2)}, u32[]{:S(2)}) async-start(bf16[64,8,4096]{2,0,1:T(8,128)(2,1)} %bitcast.37), calls=%async_computation.2 | async-start | bytes 8388608 | tf_op jit(solution)/shard_map/all_to_all | solution.py:45
  255.8 0.3 reduce-scatter.2.cloned.1.call-start
  256.7 0.0 all-gather.2.cloned.1.call-done
  256.7 0.0 copy-start.2
  256.7 22.6 %fusion.1 = f32[192,8]{0,1:T(8,128)S(1)} fusion(f32[8,32768]{1,0:T(8,128)S(1)} %copy-done, bf16[192,32768]{1,0:T(8,128)(2,1)} %all-gather.2.cloned.1.call-done), kind=kOutput, calls=%fused_computation.5 | convolution fusion | flops 616562688 | bytes 13637632 | tf_op jit(solution)/shard_map/dot_general | solution.py:35
  279.3 0.0 copy-done.2
  279.3 8.7 %fusion.22 = f32[64,192]{1,0:T(8,128)S(1)} fusion(bf16[64,32768]{1,0:T(8,128)(2,1)S(1)} %copy-done.2, bf16[192,32768]{1,0:T(8,128)(2,1)} %all-gather.2.cloned.1.call-done), kind=kOutput, calls=%fused_computation.44 | convolution fusion | flops 805306368 | bytes 16826368 | tf_op jit(solution)/shard_map/dot_general | solution.py:33
  288.0 0.3 fusion.21
  288.3 0.2 fusion.8
  288.5 0.1 fusion.19
  288.6 68.2 %all_gather.7 = bf16[512,192]{1,0:T(8,128)(2,1)S(1)} all-gather(bf16[64,192]{1,0:T(8,128)(2,1)S(1)} %get-tuple-element.5), channel_id=1, replica_groups=mesh['grp'=8,'blk'=4] {'grp'}, dimensions={0}, use_global_device_ids=true | all-gather | bytes 221184 | tf_op jit(solution)/shard_map/all_gather | solution.py:46
  356.8 0.0 all-to-all-done.2
  356.8 4.9 %fusion.23 = f32[192,4096]{1,0:T(8,128)} fusion(bf16[512,192]{1,0:T(8,128)(2,1)S(1)} %all_gather.7, bf16[512,4096]{1,0:T(8,128)(2,1)} %bitcast.11), kind=kOutput, calls=%fused_computation.45 | convolution fusion | flops 805306368 | bytes 7536640 | tf_op jit(solution)/shard_map/dot_general | solution.py:48
  361.7 0.0 reduce-scatter.2.cloned.1.call-update
  361.7 0.2 fusion.10
  362.0 39.1 %psum.7 = f32[192,8]{0,1:T(8,128)S(1)} all-reduce(f32[192,8]{0,1:T(8,128)S(1)} %fusion.10), channel_id=1, replica_groups=mesh['grp'=8,'blk'=4] {'grp','blk'}, use_global_device_ids=true, to_apply=%region_6.7 | all-reduce | flops 1536 | bytes 12288 | tf_op jit(solution)/shard_map/psum | solution.py:42
  401.1 4.8 %reduce-scatter.2.cloned.1.call-done = f32[48,4096]{1,0:T(8,128)} async-done(((f32[192,4096]{1,0:T(8,128)}), f32[48,4096]{1,0:T(8,128)}) %reduce-scatter.2.cloned.1.call-update) | async-done | bytes 786448 | tf_op jit(solution)/shard_map/reduce_scatter | solution.py:47
  405.8 2.9 fusion.4
  (4 shorter events, 0.0 us)
Async XLA Ops:
  6.5 234.9 %copy-start = (f32[8,32768]{1,0:T(8,128)S(1)}, f32[8,32768]{1,0:T(8,128)}, u32[]{:S(2)}) copy-start(f32[8,32768]{1,0:T(8,128)} %param.13) | copy-start | bytes 3145732
  19.7 9.8 %all-to-all-start = ((s32[4,1,32]{2,1,0:T(1,128)}), s32[4,1,32]{2,1,0:T(1,128)S(1)}, u32[]{:S(2)}, u32[]{:S(2)}) async-start(s32[4,1,32]{2,1,0:T(1,128)} %bitcast.4), calls=%async_computation | async-start | bytes 4096 | tf_op jit(solution)/shard_map/all_to_all | solution.py:20
  24.9 231.8 %all-gather.2.cloned.1.call-start = ((), (), s32[]{:S(2)}) async-start(), calls=%async_computation.4 | async-start | bytes 15728640 | tf_op jit(solution)/shard_map/all_gather | solution.py:32
  229.3 12.2 %copy-start.3 = (s32[64]{0:T(128)S(1)}, s32[64]{0:T(128)}, u32[]{:S(2)}) copy-start(s32[64]{0:T(128)} %param.10) | copy-start | bytes 772
  247.0 2.0 copy-start.1
  251.2 105.6 %all-to-all-start.2 = ((bf16[64,8,4096]{2,0,1:T(8,128)(2,1)}), bf16[64,8,4096]{2,0,1:T(8,128)(2,1)}, u32[]{:S(2)}, u32[]{:S(2)}) async-start(bf16[64,8,4096]{2,0,1:T(8,128)(2,1)} %bitcast.37), calls=%async_computation.2 | async-start | bytes 8388608 | tf_op jit(solution)/shard_map/all_to_all | solution.py:45
  255.8 150.1 %reduce-scatter.2.cloned.1.call-start = ((), (), s32[]{:S(2)}) async-start(), calls=%async_computation.5 | async-start | bytes 3932160 | tf_op jit(solution)/shard_map/reduce_scatter | solution.py:47
  256.7 22.6 %copy-start.2 = (bf16[64,32768]{1,0:T(8,128)(2,1)S(1)}, bf16[64,32768]{1,0:T(8,128)(2,1)}, u32[]{:S(2)}) copy-start(bf16[64,32768]{1,0:T(8,128)(2,1)} %copy-done.1) | copy-start | bytes 12582916
Sparse Core Ops, SparseCore 0:
  27.5 206.4 all-gather.1
  361.8 43.9 reduce-scatter.1
where the time goes:
time: 416 us
  blocking collectives  279 us (67%)
  local copies, waits for them, and re-layouts  46.8 us (11%)
  matrix products  45.2 us (11%)
  between operations  14.1 us (3%)
  other arithmetic  10.8 us (3%)
  starting transfers between devices  10 us (2%)
  waiting for transfers between devices  9.39 us (2%)
    all_to_all x1, blocking collectives, per_device(): lax.all_to_all(blocks_out, 'blk', split_axis=0, concat_axis=0, tiled=True)  172 us
    all_gather x1, blocking collectives, per_device(): all_weights = lax.all_gather(weighted_b, 'grp', axis=0, tiled=True)  68.2 us
    psum x1, blocking collectives, per_device(): lax.psum(jnp.dot(weighted.T, masks_hot, precision=highest), ('grp', 'blk'))  39.1 us
    dot_general x1, matrix products, per_device(): jnp.dot(wedge, (piece_float * piece_float).T, precision=highest)  22.6 us
    gather x1, local copies, waits for them, and re-layouts, per_device(): jnp.take(slab, wanted.reshape(-1), axis=0)  19.2 us
    gather x1, local copies, waits for them, and re-layouts, per_device(): blocks = fetched[owners, slot_rank]  12.2 us
    scatter x1, local copies, waits for them, and re-layouts, per_device(): jnp.zeros((cycle_size, capacity), jnp.int32).at[owners, slot_rank]  10.1 us
    dot_general x1, matrix products, per_device(): correl = jnp.dot(scaled, ref_piece.T, preferred_element_type=jnp.float32)  8.69 us
  transfers between devices with their start and end apart: 4, of which 2 were waited for; matrix products, arithmetic and copies ran while one was open for 19% of the time, Pallas kernels for 0%

commit v1 on v0

--- a/solution.py
+++ b/solution.py
@@ -39,7 +39,7 @@
     live_mask = (jnp.arange(slot_count, dtype=jnp.int32) < live_count[0]).astype(jnp.float32)
     weighted = posterior * live_mask[:, None]
     weighted_b = weighted.astype(jnp.bfloat16)
-    totals = lax.psum(jnp.dot(weighted.T, masks_hot, precision=highest), ("grp", "blk"))
+    totals = lax.psum(lax.psum(jnp.dot(weighted.T, masks_hot, precision=highest), "blk"), "grp")
     per_vox = voxels // group_count
     contract = (((0,), (0,)), ((), ()))
     columns = lax.all_to_all(scaled, "grp", split_axis=1, concat_axis=0, tiled=True)

time: 416 us -> 416 us (level)
  blocking collectives: 279 us -> 263 us
  waiting for transfers between devices: 9.39 us -> 24.3 us
    psum x1 -> x2, blocking collectives: 39.1 us -> 23.4 us  [the longest x1 14.2 us: per_device(): lax.psum(lax.psum(jnp.dot(weighted.T, masks_hot, precision=highest), 'blk...]
    reduce_scatter x1, waiting for transfers between devices: 4.76 us -> 19.7 us  [per_device(): lax.psum_scatter(lax.dot_general(all_weights, columns, contract, preferre...]
where the time goes in v1:
time: 416 us; the launch traced here: 415 us
  blocking collectives  263 us (63%)
  local copies, waits for them, and re-layouts  46.8 us (11%)
  matrix products  45.2 us (11%)
  waiting for transfers between devices  24.3 us (6%)
  between operations  14.2 us (3%)
  other arithmetic  10.8 us (3%)
  starting transfers between devices  10 us (2%)
    all_to_all x1, blocking collectives, per_device(): lax.all_to_all(blocks_out, 'blk', split_axis=0, concat_axis=0, tiled=True)  172 us
    all_gather x1, blocking collectives, per_device(): all_weights = lax.all_gather(weighted_b, 'grp', axis=0, tiled=True)  68.2 us
    dot_general x1, matrix products, per_device(): jnp.dot(wedge, (piece_float * piece_float).T, precision=highest)  22.6 us
    reduce_scatter x1, waiting for transfers between devices, per_device(): lax.psum_scatter(lax.dot_general(all_weights, columns, contract, preferre...  19.7 us
    gather x1, local copies, waits for them, and re-layouts, per_device(): jnp.take(slab, wanted.reshape(-1), axis=0)  19.2 us
    psum x1, blocking collectives, per_device(): lax.psum(lax.psum(jnp.dot(weighted.T, masks_hot, precision=highest), 'blk...  14.2 us
    gather x1, local copies, waits for them, and re-layouts, per_device(): blocks = fetched[owners, slot_rank]  12.2 us
    scatter x1, local copies, waits for them, and re-layouts, per_device(): jnp.zeros((cycle_size, capacity), jnp.int32).at[owners, slot_rank]  10.1 us
  transfers between devices with their start and end apart: 4, of which 2 were waited for; matrix products, arithmetic and copies ran while one was open for 19% of the time, Pallas kernels for 0%

profile of v1, /device:TPU:0, one launch (start us, length us, event | category | flops | bytes accessed | tf_op | source)
XLA Modules:
  0.0 414.9 jit_solution(16535165400571054729)
XLA Ops:
  6.5 0.0 copy-start
  6.5 0.8 fusion.9
  7.4 0.1 reduce_window_sum.11
  7.4 0.8 select_reduce_fusion
  8.3 0.7 fusion.18
  9.0 0.6 broadcast_in_dim.12
  9.5 10.1 %scatter_fusion = s32[4,32]{1,0:T(4,128)} fusion(s32[4,32]{1,0:T(4,128)} %broadcast_in_dim.12, s32[64]{0:T(128)S(1)} %get-tuple-element.7, s32[64]{0:T(128)} %param.9), kind=kCustom, calls=%fused_computation.2 | custom fusion | bytes 1280 | tf_op jit(solution)/shard_map/scatter | solution.py:19
  19.7 5.2 %all-to-all-start = ((s32[4,1,32]{2,1,0:T(1,128)}), s32[4,1,32]{2,1,0:T(1,128)S(1)}, u32[]{:S(2)}, u32[]{:S(2)}) async-start(s32[4,1,32]{2,1,0:T(1,128)} %bitcast.4), calls=%async_computation | async-start | bytes 4096 | tf_op jit(solution)/shard_map/all_to_all | solution.py:20
  24.9 0.0 all-gather.2.cloned.1.call-start
  24.9 0.7 all-gather.2.cloned.1.call-update
  25.6 3.9 all-to-all-done
  29.5 0.5 broadcast.140
  30.0 0.7 reduce.3
  30.6 0.1 reshape.75
  30.7 19.2 %gather_fusion = bf16[128,32768]{1,0:T(8,128)(2,1)} fusion(bf16[64,32768]{1,0:T(8,128)(2,1)} %param.7, s32[1024]{0:T(1024)S(1)} %pad_clamp_fusion), kind=kCustom, calls=%fused_computation | custom fusion | bytes 16777728 | tf_op jit(solution)/shard_map/jit(_take)/gather | solution.py:22
  49.9 7.4 %broadcast_select_fusion = bf16[4,32,32768]{2,1,0:T(8,128)(2,1)} fusion(bf16[4,32,32768]{2,1,0:T(8,128)(2,1)} %bitcast.36, pred[4,32]{1,0:T(4,128)(4,1)S(1)} %compare_and_fusion), kind=kLoop, calls=%fused_computation.8 | loop fusion | flops 4194304 | bytes 16777344 | tf_op jit(solution)/shard_map/jit(_take)/select_n | solution.py:22
  57.4 171.9 %all_to_all.33 = bf16[4,32,32768]{2,1,0:T(8,128)(2,1)} all-to-all(bf16[4,32,32768]{2,1,0:T(8,128)(2,1)} %broadcast_select_fusion), channel_id=1, replica_groups=mesh['grp'=8,'blk'=4] {'blk'}, dimensions={0} | all-to-all | bytes 16777216 | tf_op jit(solution)/shard_map/all_to_all | solution.py:23
  229.3 0.0 copy-start.3
  229.3 12.2 %gather_fusion.1 = bf16[64,32768]{1,0:T(8,128)(2,1)} fusion(bf16[4,32,32768]{2,1,0:T(8,128)(2,1)} %all_to_all.33, s32[64]{0:T(128)S(1)} %bitcast.38), kind=kCustom, calls=%fused_computation.1 | custom fusion | bytes 8389120 | tf_op jit(solution)/shard_map/gather | solution.py:24
  241.5 0.0 copy-done
  241.5 0.0 copy-done.3
  241.5 5.5 %fusion = bf16[64,32768]{1,0:T(8,128)(2,1)S(1)} fusion(f32[8,32768]{1,0:T(8,128)S(1)} %copy-done, bf16[64,32768]{1,0:T(8,128)(2,1)} %gather_fusion.1, s32[64]{0:T(128)S(1)} %copy-done.3), kind=kOutput, calls=%fused_computation.4 | convolution fusion | flops 207618560 | bytes 9437440 | tf_op jit(solution)/shard_map/dot_general | solution.py:28
  247.0 0.0 copy-start.1
  247.0 2.0 copy-done.1
  249.0 2.2 copy.13
  251.2 4.6 %all-to-all-start.2 = ((bf16[64,8,4096]{2,0,1:T(8,128)(2,1)}), bf16[64,8,4096]{2,0,1:T(8,128)(2,1)}, u32[]{:S(2)}, u32[]{:S(2)}) async-start(bf16[64,8,4096]{2,0,1:T(8,128)(2,1)} %bitcast.37), calls=%async_computation.2 | async-start | bytes 8388608 | tf_op jit(solution)/shard_map/all_to_all | solution.py:45
  255.8 0.3 reduce-scatter.2.cloned.1.call-start
  256.7 0.0 all-gather.2.cloned.1.call-done
  256.7 0.0 copy-start.2
  256.7 22.6 %fusion.1 = f32[192,8]{0,1:T(8,128)S(1)} fusion(f32[8,32768]{1,0:T(8,128)S(1)} %copy-done, bf16[192,32768]{1,0:T(8,128)(2,1)} %all-gather.2.cloned.1.call-done), kind=kOutput, calls=%fused_computation.5 | convolution fusion | flops 616562688 | bytes 13637632 | tf_op jit(solution)/shard_map/dot_general | solution.py:35
  279.3 0.0 copy-done.2
  279.3 8.7 %fusion.22 = f32[64,192]{1,0:T(8,128)S(1)} fusion(bf16[64,32768]{1,0:T(8,128)(2,1)S(1)} %copy-done.2, bf16[192,32768]{1,0:T(8,128)(2,1)} %all-gather.2.cloned.1.call-done), kind=kOutput, calls=%fused_computation.44 | convolution fusion | flops 805306368 | bytes 16826368 | tf_op jit(solution)/shard_map/dot_general | solution.py:33
  288.0 0.3 fusion.21
  288.3 0.2 fusion.8
  288.5 0.1 fusion.19
  288.6 68.2 %all_gather.7 = bf16[512,192]{1,0:T(8,128)(2,1)S(1)} all-gather(bf16[64,192]{1,0:T(8,128)(2,1)S(1)} %get-tuple-element.5), channel_id=1, replica_groups=mesh['grp'=8,'blk'=4] {'grp'}, dimensions={0}, use_global_device_ids=true | all-gather | bytes 221184 | tf_op jit(solution)/shard_map/all_gather | solution.py:46
  356.8 0.0 all-to-all-done.2
  356.8 4.9 %fusion.23 = f32[192,4096]{1,0:T(8,128)} fusion(bf16[512,192]{1,0:T(8,128)(2,1)S(1)} %all_gather.7, bf16[512,4096]{1,0:T(8,128)(2,1)} %bitcast.11), kind=kOutput, calls=%fused_computation.45 | convolution fusion | flops 805306368 | bytes 7536640 | tf_op jit(solution)/shard_map/dot_general | solution.py:48
  361.7 0.0 reduce-scatter.2.cloned.1.call-update
  361.7 0.2 fusion.10
  362.0 9.2 %psum.14 = f32[192,8]{0,1:T(8,128)S(1)} all-reduce(f32[192,8]{0,1:T(8,128)S(1)} %fusion.10), channel_id=1, replica_groups=mesh['grp'=8,'blk'=4] {'blk'}, use_global_device_ids=true, to_apply=%region_6.7 | all-reduce | flops 1536 | bytes 12288 | tf_op jit(solution)/shard_map/psum | solution.py:42
  371.1 14.2 %psum.15 = f32[192,8]{0,1:T(8,128)S(1)} all-reduce(f32[192,8]{0,1:T(8,128)S(1)} %psum.14), channel_id=1, replica_groups=mesh['grp'=8,'blk'=4] {'grp'}, use_global_device_ids=true, to_apply=%region_7.8 | all-reduce | flops 1536 | bytes 12288 | tf_op jit(solution)/shard_map/psum | solution.py:42
  385.4 19.7 %reduce-scatter.2.cloned.1.call-done = f32[48,4096]{1,0:T(8,128)} async-done(((f32[192,4096]{1,0:T(8,128)}), f32[48,4096]{1,0:T(8,128)}) %reduce-scatter.2.cloned.1.call-update) | async-done | bytes 786448 | tf_op jit(solution)/shard_map/reduce_scatter | solution.py:47
  405.1 2.9 fusion.4
  (4 shorter events, 0.0 us)
Async XLA Ops:
  6.5 234.9 %copy-start = (f32[8,32768]{1,0:T(8,128)S(1)}, f32[8,32768]{1,0:T(8,128)}, u32[]{:S(2)}) copy-start(f32[8,32768]{1,0:T(8,128)} %param.13) | copy-start | bytes 3145732
  19.7 9.8 %all-to-all-start = ((s32[4,1,32]{2,1,0:T(1,128)}), s32[4,1,32]{2,1,0:T(1,128)S(1)}, u32[]{:S(2)}, u32[]{:S(2)}) async-start(s32[4,1,32]{2,1,0:T(1,128)} %bitcast.4), calls=%async_computation | async-start | bytes 4096 | tf_op jit(solution)/shard_map/all_to_all | solution.py:20
  24.9 231.8 %all-gather.2.cloned.1.call-start = ((), (), s32[]{:S(2)}) async-start(), calls=%async_computation.4 | async-start | bytes 15728640 | tf_op jit(solution)/shard_map/all_gather | solution.py:32
  229.3 12.2 %copy-start.3 = (s32[64]{0:T(128)S(1)}, s32[64]{0:T(128)}, u32[]{:S(2)}) copy-start(s32[64]{0:T(128)} %param.10) | copy-start | bytes 772
  247.0 2.0 copy-start.1
  251.2 105.6 %all-to-all-start.2 = ((bf16[64,8,4096]{2,0,1:T(8,128)(2,1)}), bf16[64,8,4096]{2,0,1:T(8,128)(2,1)}, u32[]{:S(2)}, u32[]{:S(2)}) async-start(bf16[64,8,4096]{2,0,1:T(8,128)(2,1)} %bitcast.37), calls=%async_computation.2 | async-start | bytes 8388608 | tf_op jit(solution)/shard_map/all_to_all | solution.py:45
  255.8 149.3 %reduce-scatter.2.cloned.1.call-start = ((), (), s32[]{:S(2)}) async-start(), calls=%async_computation.5 | async-start | bytes 3932160 | tf_op jit(solution)/shard_map/reduce_scatter | solution.py:47
  256.7 22.6 %copy-start.2 = (bf16[64,32768]{1,0:T(8,128)(2,1)S(1)}, bf16[64,32768]{1,0:T(8,128)(2,1)}, u32[]{:S(2)}) copy-start(bf16[64,32768]{1,0:T(8,128)(2,1)} %copy-done.1) | copy-start | bytes 12582916
Sparse Core Ops, SparseCore 0:
  27.5 206.4 all-gather.1
  361.8 43.2 reduce-scatter.1
